TPU v7x, 512 devices: a whole 4x4x16 slice. The times are simulated.
512 devices in a mesh: rows: 128 (over x, z, core), rep: 4 (over y).
Axes of the slice: x: 4, y: 4, z: 16, core: 2. Of those that a mesh axis runs over, the one named last changes fastest.
Arguments:
- feats: bfloat16 [4, 32768, 512], P('rep', 'rows'), may hold values from -24 to 24
- grad_out: bfloat16 [4, 32768, 512], P('rep', 'rows'), may hold values from -6 to 6
- qkv_weight: bfloat16 [512, 1536], P('rows'), may hold values from -0.25 to 0.25
- proj_weight: bfloat16 [512, 512], P('rows'), may hold values from -0.25 to 0.25
- to_hilbert: int32 [4, 16384], P('rep', 'rows'), may hold values from 0 to 16383, as said below
- to_zorder: int32 [4, 16384], P('rep', 'rows'), may hold values from 0 to 16383, as said below
Outputs:
- grad_feats: bfloat16 [4, 32768, 512], P('rep', 'rows')
- qkv_grad: float32 [512, 1536], P('rows')
- proj_grad: float32 [512, 512], P('rows')
Inputs may be any that keep to these rules, and one draw needn't show every extreme that they name: to_hilbert[s] is a permutation of the blocks of scene s and to_zorder[s] its inverse; of the 128 Z-order blocks of one device, at most 2 have Hilbert positions on any one device, and exactly 2 for some pair of devices in every scene. `to_zorder`: the inverse of to_hilbert in every scene.
All inputs are finite; a program needn't handle non-finite values.
Results may differ from a plain program's by a relative error of at most 0.015.
The roundings to bfloat16 on the way count: a program that leaves them out, or rounds other values in their place, can miss the bound.
Values may be sent and summed in bfloat16 or wider, within the bound.
No kernel may reach another device: no remote copies, remote signals or barrier semaphores. Data moves between devices by JAX's collectives and lax.ppermute only.
A program may use at most 64 MiB of HBM per device.

v0:
```python
import jax
import jax.numpy as jnp
from jax import lax
from jax.sharding import PartitionSpec as P

HEADS = 8
CAP = 2


def from_partner(block, axis, apart):
    count = lax.axis_size(axis)
    route = []
    for low in range(count):
        high = low | 1 << apart
        if high != low and high < count:
            route += [(low, high), (high, low)]
    return lax.ppermute(block, axis, route)


def move_blocks(outgoing):
    return lax.all_to_all(outgoing, "rows", split_axis=0, concat_axis=0, tiled=True)


def rank_within(order_keys, owners):
    same_owner = owners[None, :] == owners[:, None]
    earlier = order_keys[None, :] < order_keys[:, None]
    return jnp.sum(jnp.logical_and(same_owner, earlier).astype(jnp.int32), axis=1)


def contract_rows(left, right):
    return lax.dot_general(
        left, right, (((0,), (0,)), ((), ())), preferred_element_type=jnp.float32
    )


def contract_cols(left, right):
    return lax.dot_general(
        left, right, (((1,), (1,)), ((), ())), preferred_element_type=jnp.float32
    )


def per_device(feats, grad_out, qkv_weight, proj_weight, to_hilbert, to_zorder):
    peer_count = lax.axis_size("rows")
    feature = feats[0]
    rows_dev, channels = feature.shape
    head_size = channels // HEADS
    scale = head_size ** (-0.5)
    blocks_dev = to_hilbert.shape[1]
    slot_count = peer_count * CAP
    w_qkv, w_proj = (
        lax.all_gather(qkv_weight, "rows", axis=0, tiled=True),
        lax.all_gather(proj_weight, "rows", axis=0, tiled=True),
    )
    forward_list = to_hilbert[0]
    inverse_list = to_zorder[0]
    local_ids = jnp.arange(blocks_dev, dtype=jnp.int32)
    slot_ids = jnp.arange(slot_count, dtype=jnp.int32)
    target_dev = forward_list // blocks_dev
    send_slot = target_dev * CAP + rank_within(local_ids, target_dev)
    send_table = (send_slot[None, :] == slot_ids[:, None]).astype(jnp.bfloat16)
    source_dev = inverse_list // blocks_dev
    recv_slot = source_dev * CAP + rank_within(inverse_list, source_dev)
    recv_table = (recv_slot[:, None] == slot_ids[None, :]).astype(jnp.bfloat16)
    zblocks = grad_out[0].reshape(blocks_dev, -1)
    outgoing = jnp.dot(send_table, zblocks, preferred_element_type=jnp.float32).astype(jnp.bfloat16)
    arrived = move_blocks(outgoing.reshape(peer_count, CAP, -1)).reshape(slot_count, -1)
    grad_hil = jnp.dot(recv_table, arrived, preferred_element_type=jnp.float32).astype(jnp.bfloat16)
    grad_hil = grad_hil.reshape(rows_dev, channels)
    qkv = jnp.dot(feature, w_qkv, preferred_element_type=jnp.float32).astype(jnp.bfloat16)
    query = qkv[:, :channels]
    keyval = qkv[:, channels:]
    grad_attn = contract_cols(grad_hil, w_proj).astype(jnp.bfloat16)
    other_kv = from_partner(keyval, "rows", 0)
    keys_all = jnp.concatenate([keyval[:, :channels], other_kv[:, :channels]], axis=0)
    values_all = jnp.concatenate([keyval[:, channels:], other_kv[:, channels:]], axis=0)
    attn_parts, dq_parts, dk_parts, dv_parts = ([], [], [], [])
    for head_index in range(HEADS):
        lo_col = head_index * head_size
        q_head = query[:, lo_col : lo_col + head_size]
        k_head = keys_all[:, lo_col : lo_col + head_size]
        v_head = values_all[:, lo_col : lo_col + head_size]
        g_head = grad_attn[:, lo_col : lo_col + head_size]
        score = contract_cols(q_head, k_head) * scale
        row_max = jnp.max(score, axis=1, keepdims=True)
        raised = jnp.exp(score - row_max)
        row_sum = jnp.sum(raised, axis=1, keepdims=True)
        probs = raised / row_sum
        probs_b = probs.astype(jnp.bfloat16)
        attn_parts.append(
            jnp.dot(probs_b, v_head, preferred_element_type=jnp.float32).astype(jnp.bfloat16)
        )
        dprob = contract_cols(g_head, v_head)
        delta = jnp.sum(probs * dprob, axis=1, keepdims=True)
        dscore = (probs * (dprob - delta) * scale).astype(jnp.bfloat16)
        dq_parts.append(jnp.dot(dscore, k_head, preferred_element_type=jnp.float32))
        dk_parts.append(contract_rows(dscore, q_head))
        dv_parts.append(contract_rows(probs_b, g_head))
    grad_q = jnp.concatenate(dq_parts, axis=1)
    grad_k = jnp.concatenate(dk_parts, axis=1)
    grad_v = jnp.concatenate(dv_parts, axis=1)
    other_k, other_v = (
        from_partner(grad_k[rows_dev:].astype(jnp.bfloat16), "rows", 0).astype(jnp.float32),
        from_partner(grad_v[rows_dev:].astype(jnp.bfloat16), "rows", 0).astype(jnp.float32),
    )
    grad_k = grad_k[:rows_dev] + other_k
    grad_v = grad_v[:rows_dev] + other_v
    grad_qkv = jnp.concatenate([grad_q, grad_k, grad_v], axis=1).astype(jnp.bfloat16)
    attn = jnp.concatenate(attn_parts, axis=1)
    grad_hfeat = contract_cols(grad_qkv, w_qkv).astype(jnp.bfloat16)
    hblocks = grad_hfeat.reshape(blocks_dev, -1)
    going_back = contract_rows(recv_table, hblocks).astype(jnp.bfloat16)
    returned = move_blocks(going_back.reshape(peer_count, CAP, -1)).reshape(slot_count, -1)
    grad_z = contract_rows(send_table, returned).astype(jnp.bfloat16).reshape(rows_dev, channels)
    share = channels // peer_count
    term = jnp.concatenate(
        [contract_rows(feature, grad_qkv), contract_rows(attn, grad_hil)], axis=1
    )
    total = lax.psum(term, ("rows", "rep"))
    owned = lax.dynamic_slice_in_dim(total, lax.axis_index("rows") * share, share, 0)
    return (grad_z[None], owned[:, : 3 * channels], owned[:, 3 * channels :])


def solution(mesh):
    placed = (
        P("rep", "rows", None),
        P("rep", "rows", None),
        P("rows", None),
        P("rows", None),
        P("rep", "rows"),
        P("rep", "rows"),
    )
    return jax.shard_map(
        per_device,
        mesh=mesh,
        in_specs=placed,
        out_specs=(P("rep", "rows", None), P("rows", None), P("rows", None)),
        check_vma=False,
    )
```

profile of v0, /device:TPU:2, one launch (start us, length us, event | category | flops | bytes accessed | tf_op | source)
XLA Modules:
  0.0 721.0 jit_solution(14029525855574183305)
XLA Ops:
  7.9 1.0 reshape_squeeze.3
  11.5 1.0 reshape.119
  12.5 19.5 %all-to-all-start = ((bf16[128,2,1024]{2,1,0:T(2,128)(2,1)}), bf16[128,2,1024]{2,1,0:T(2,128)(2,1)S(1)}, u32[]{:S(2)}, u32[]{:S(2)}) async-start(bf16[128,2,1024]{2,1,0:T(2,128)(2,1)} %reshape.119), calls=%async_computation | async-start | bytes 1048576 | tf_op jit(solution)/shard_map/all_to_all | solution.py:21
  32.0 100.5 %all-gather.1 = bf16[128,4,512]{2,1,0:T(4,128)(2,1)S(1)} all-gather(bf16[1,4,512]{2,1,0:T(4,128)(2,1)S(1)} %bitcast.64), channel_id=1, replica_groups=mesh['rows'=128,'rep'=4] {'rows'}, dimensions={0}, use_global_device_ids=true | all-gather | bytes 528384 | tf_op jit(solution)/shard_map/all_gather | solution.py:52
  132.9 1.0 reshape.120
  133.9 22.9 %all-gather.4.cloned.1.call-done = bf16[128,4,1536]{2,1,0:T(4,128)(2,1)} async-done(((bf16[1,4,1536]{2,1,0:T(4,128)(2,1)}), bf16[128,4,1536]{2,1,0:T(4,128)(2,1)}) %all-gather.4.cloned.1.call-update) | async-done | bytes 1572880 | tf_op jit(solution)/shard_map/all_gather | solution.py:51
  156.9 2.7 reshape.126
  161.0 2.3 collective-permute-start
  164.4 1.0 reshape.121
  165.8 1.1 fusion.160
  180.5 2.1 collective-permute-start.2
  182.6 1.3 fusion.169
  188.6 2.4 collective-permute-start.1
  192.2 1.3 convolution_convert_fusion.4
  194.1 1.7 reshape.122
  195.8 2.2 convolution_convert_fusion.1
  198.0 2.1 reshape.123
  200.1 12.8 %all-to-all-start.1 = ((bf16[128,2,1024]{2,1,0:T(2,128)(2,1)}), bf16[128,2,1024]{2,1,0:T(2,128)(2,1)}, u32[]{:S(2)}, u32[]{:S(2)}) async-start(bf16[128,2,1024]{2,1,0:T(2,128)(2,1)} %reshape.123), calls=%async_computation.1 | async-start | bytes 1048576 | tf_op jit(solution)/shard_map/all_to_all | solution.py:21
  212.9 3.6 pad_maximum_fusion
  216.5 29.6 %all-to-all-done.1 = bf16[128,2,1024]{2,1,0:T(2,128)(2,1)} async-done(((bf16[128,2,1024]{2,1,0:T(2,128)(2,1)}), bf16[128,2,1024]{2,1,0:T(2,128)(2,1)}, u32[]{:S(2)}, u32[]{:S(2)}) %all-to-all-start.1) | async-done | bytes 524320 | tf_op jit(solution)/shard_map/all_to_all | solution.py:21
  246.2 1.2 reshape.124
  248.5 461.6 %all-reduce.2.cloned.1.call-done = f32[512,2048]{0,1:T(8,128)} async-done(((f32[512,2048]{0,1:T(8,128)}), f32[512,2048]{0,1:T(8,128)}) %all-reduce.2.cloned.1.call-update) | async-done | bytes 4194320 | tf_op jit(solution)/shard_map/psum | solution.py:118
  710.0 1.4 constant_dynamic-slice_fusion
  712.3 1.1 dynamic-slice.1
  (106 shorter events, 28.9 us)
Async XLA Ops:
  7.2 152.4 %copy-start = (bf16[1,256,512]{2,1,0:T(8,128)(2,1)S(1)}, bf16[1,256,512]{2,1,0:T(8,128)(2,1)}, u32[]{:S(2)}) copy-start(bf16[1,256,512]{2,1,0:T(8,128)(2,1)} %param.6) | copy-start | bytes 786436
  7.2 24.8 %copy-start.2 = (bf16[4,512]{1,0:T(4,128)(2,1)S(1)}, bf16[4,512]{1,0:T(4,128)(2,1)}, u32[]{:S(2)}) copy-start(bf16[4,512]{1,0:T(4,128)(2,1)} %param.9) | copy-start | bytes 12292
  7.2 125.5 %copy-start.3 = (s32[1,128]{1,0:T(1,128)S(1)}, s32[1,128]{1,0:T(1,128)}, u32[]{:S(2)}) copy-start(s32[1,128]{1,0:T(1,128)} %param.11) | copy-start | bytes 1540
  7.2 149.7 %all-gather.4.cloned.1.call-start = ((), (), s32[]{:S(2)}) async-start(), calls=%async_computation.3 | async-start | bytes 1585152 | tf_op jit(solution)/shard_map/all_gather | solution.py:51
  12.5 120.5 %all-to-all-start = ((bf16[128,2,1024]{2,1,0:T(2,128)(2,1)}), bf16[128,2,1024]{2,1,0:T(2,128)(2,1)S(1)}, u32[]{:S(2)}, u32[]{:S(2)}) async-start(bf16[128,2,1024]{2,1,0:T(2,128)(2,1)} %reshape.119), calls=%async_computation | async-start | bytes 1048576 | tf_op jit(solution)/shard_map/all_to_all | solution.py:21
  159.6 3.8 copy-start.1
  161.0 4.8 collective-permute-start
  180.5 11.7 %collective-permute-start.2 = (bf16[256,512]{0,1:T(8,128)(2,1)S(1)}, bf16[256,512]{0,1:T(8,128)(2,1)S(1)}, u32[]{:S(2)}, u32[]{:S(2)}) collective-permute-start(bf16[256,512]{0,1:T(8,128)(2,1)S(1)} %slice.454), channel_id=1, source_target_pairs={{0,4},{4,0},{8,12},{12,8},{16,20},{20,16},{24,28},{28,24},{32,36},... | collective-permute-start | bytes 786440 | tf_op jit(solution)/shard_map/ppermute | solution.py:17
  188.6 3.4 collective-permute-start.1
  200.1 46.1 %all-to-all-start.1 = ((bf16[128,2,1024]{2,1,0:T(2,128)(2,1)}), bf16[128,2,1024]{2,1,0:T(2,128)(2,1)}, u32[]{:S(2)}, u32[]{:S(2)}) async-start(bf16[128,2,1024]{2,1,0:T(2,128)(2,1)} %reshape.123), calls=%async_computation.1 | async-start | bytes 1048576 | tf_op jit(solution)/shard_map/all_to_all | solution.py:21
  212.9 497.2 %all-reduce.2.cloned.1.call-start = ((), (), s32[]{:S(2)}) async-start(), calls=%async_computation.2 | async-start | bytes 8388608 | tf_op jit(solution)/shard_map/psum | solution.py:118
Sparse Core Ops, SparseCore 0:
  11.1 145.7 all-gather.3
  219.2 490.8 all-reduce.1
where the time goes:
time: 722 us; the launch traced here: 721 us
  waiting for transfers between devices  515 us (71%)
  blocking collectives  101 us (14%)
  starting transfers between devices  39.3 us (5%)
  matrix products  22.5 us (3%)
  local copies, waits for them, and re-layouts  18.9 us (3%)
  between operations  14.4 us (2%)
  other arithmetic  9.94 us (1%)
    psum x1, waiting for transfers between devices, per_device(): total = lax.psum(term, ('rows', 'rep'))  462 us
    all_gather x1, blocking collectives, per_device(): lax.all_gather(proj_weight, 'rows', axis=0, tiled=True)  101 us
    all_to_all x2, starting transfers between devices, move_blocks(): lax.all_to_all(outgoing, 'rows', split_axis=0, concat_axis=0, tiled=True)  32.3 us
    all_to_all x2, waiting for transfers between devices, move_blocks(): lax.all_to_all(outgoing, 'rows', split_axis=0, concat_axis=0, tiled=True)  29.6 us
    all_gather x1, waiting for transfers between devices, per_device(): lax.all_gather(qkv_weight, 'rows', axis=0, tiled=True)  22.9 us
  transfers between devices with their start and end apart: 7, of which 4 were waited for; matrix products, arithmetic and copies ran while one was open for 3% of the time, Pallas kernels for 0%

commit v1 on v0

--- a/solution.py
+++ b/solution.py
@@ -115,7 +115,10 @@
     term = jnp.concatenate(
         [contract_rows(feature, grad_qkv), contract_rows(attn, grad_hil)], axis=1
     )
-    total = lax.psum(term, ("rows", "rep"))
+    _divide_state = lambda row_axis, named_axis, load: lax.psum(
+        lax.psum(load, named_axis), row_axis
+    )
+    total = _divide_state("rows", "rep", term)
     owned = lax.dynamic_slice_in_dim(total, lax.axis_index("rows") * share, share, 0)
     return (grad_z[None], owned[:, : 3 * channels], owned[:, 3 * channels :])
 

time: 722 us -> 674 us (0.934)
  the two profiles are of different devices: /device:TPU:2 before, /device:TPU:8 now
where the time goes in v1:
time: 674 us
  waiting for transfers between devices  476 us (71%)
  blocking collectives  100 us (15%)
  starting transfers between devices  38.4 us (6%)
  matrix products  19 us (3%)
  local copies, waits for them, and re-layouts  17.2 us (3%)
  between operations  14.2 us (2%)
  other arithmetic  8.77 us (1%)
    psum x1, waiting for transfers between devices, per_device(): lax.psum(lax.psum(load, named_axis), row_axis)  362 us
    all_gather x1, blocking collectives, per_device(): lax.all_gather(proj_weight, 'rows', axis=0, tiled=True)  100 us
    psum x1, waiting for transfers between devices, per_device(): lax.psum(load, named_axis)  88.4 us
    all_to_all x2, starting transfers between devices, move_blocks(): lax.all_to_all(outgoing, 'rows', split_axis=0, concat_axis=0, tiled=True)  31.4 us
    all_gather x1, waiting for transfers between devices, per_device(): lax.all_gather(qkv_weight, 'rows', axis=0, tiled=True)  23.7 us
  transfers between devices with their start and end apart: 8, of which 4 were waited for; matrix products, arithmetic and copies ran while one was open for 3% of the time, Pallas kernels for 0%

profile of v1, /device:TPU:8, one launch (start us, length us, event | category | flops | bytes accessed | tf_op | source)
XLA Modules:
  0.0 673.5 jit_solution(1191052155098083015)
XLA Ops:
  7.9 1.0 reshape_squeeze.3
  11.5 1.0 reshape.119
  12.5 19.8 %all-to-all-start = ((bf16[128,2,1024]{2,1,0:T(2,128)(2,1)}), bf16[128,2,1024]{2,1,0:T(2,128)(2,1)S(1)}, u32[]{:S(2)}, u32[]{:S(2)}) async-start(bf16[128,2,1024]{2,1,0:T(2,128)(2,1)} %reshape.119), calls=%async_computation | async-start | bytes 1048576 | tf_op jit(solution)/shard_map/all_to_all | solution.py:21
  32.3 100.3 %all-gather.1 = bf16[128,4,512]{2,1,0:T(4,128)(2,1)S(1)} all-gather(bf16[1,4,512]{2,1,0:T(4,128)(2,1)S(1)} %bitcast.64), channel_id=1, replica_groups=mesh['rows'=128,'rep'=4] {'rows'}, dimensions={0}, use_global_device_ids=true | all-gather | bytes 528384 | tf_op jit(solution)/shard_map/all_gather | solution.py:52
  133.0 1.0 reshape.120
  134.0 23.7 %all-gather.4.cloned.1.call-done = bf16[128,4,1536]{2,1,0:T(4,128)(2,1)} async-done(((bf16[1,4,1536]{2,1,0:T(4,128)(2,1)}), bf16[128,4,1536]{2,1,0:T(4,128)(2,1)}) %all-gather.4.cloned.1.call-update) | async-done | bytes 1572880 | tf_op jit(solution)/shard_map/all_gather | solution.py:51
  157.7 2.7 reshape.126
  161.0 0.9 slice.187
  161.9 2.3 collective-permute-start
  164.3 1.0 convolution_convert_fusion.6
  165.2 1.0 reshape.121
  166.7 1.1 fusion.160
  181.3 2.1 collective-permute-start.2
  188.5 2.4 collective-permute-start.1
  192.1 0.9 copy-done.2
  193.6 2.4 pad_maximum_fusion
  196.1 1.1 copy-done.3
  198.3 1.0 reshape.123
  199.3 11.7 %all-to-all-start.1 = ((bf16[128,2,1024]{2,1,0:T(2,128)(2,1)}), bf16[128,2,1024]{2,1,0:T(2,128)(2,1)S(1)}, u32[]{:S(2)}, u32[]{:S(2)}) async-start(bf16[128,2,1024]{2,1,0:T(2,128)(2,1)} %reshape.123), calls=%async_computation.1 | async-start | bytes 1048576 | tf_op jit(solution)/shard_map/all_to_all | solution.py:21
  211.1 88.4 %all-reduce.3.cloned.1.call-done = f32[512,2048]{0,1:T(8,128)} async-done(((f32[512,2048]{0,1:T(8,128)}), f32[512,2048]{0,1:T(8,128)}) %all-reduce.3.cloned.1.call-update) | async-done | bytes 4194320 | tf_op jit(solution)/shard_map/psum | solution.py:119
  300.8 362.2 %all-reduce.5.cloned.1.call-done = f32[512,2048]{0,1:T(8,128)} async-done(((f32[512,2048]{0,1:T(8,128)}), f32[512,2048]{0,1:T(8,128)}) %all-reduce.5.cloned.1.call-update) | async-done | bytes 4194320 | tf_op jit(solution)/shard_map/psum | solution.py:118
  662.9 1.4 constant_dynamic-slice_fusion
  664.3 0.9 copy.13
  665.2 1.1 dynamic-slice.1
  (113 shorter events, 27.9 us)
Async XLA Ops:
  7.2 153.3 %copy-start = (bf16[1,256,512]{2,1,0:T(8,128)(2,1)S(1)}, bf16[1,256,512]{2,1,0:T(8,128)(2,1)}, u32[]{:S(2)}) copy-start(bf16[1,256,512]{2,1,0:T(8,128)(2,1)} %param.6) | copy-start | bytes 786436
  7.2 25.1 %copy-start.4 = (bf16[4,512]{1,0:T(4,128)(2,1)S(1)}, bf16[4,512]{1,0:T(4,128)(2,1)}, u32[]{:S(2)}) copy-start(bf16[4,512]{1,0:T(4,128)(2,1)} %param.9) | copy-start | bytes 12292
  7.2 125.6 %copy-start.5 = (s32[1,128]{1,0:T(1,128)S(1)}, s32[1,128]{1,0:T(1,128)}, u32[]{:S(2)}) copy-start(s32[1,128]{1,0:T(1,128)} %param.11) | copy-start | bytes 1540
  7.2 150.5 %all-gather.4.cloned.1.call-start = ((), (), s32[]{:S(2)}) async-start(), calls=%async_computation.4 | async-start | bytes 1585152 | tf_op jit(solution)/shard_map/all_gather | solution.py:51
  12.5 120.6 %all-to-all-start = ((bf16[128,2,1024]{2,1,0:T(2,128)(2,1)}), bf16[128,2,1024]{2,1,0:T(2,128)(2,1)S(1)}, u32[]{:S(2)}, u32[]{:S(2)}) async-start(bf16[128,2,1024]{2,1,0:T(2,128)(2,1)} %reshape.119), calls=%async_computation | async-start | bytes 1048576 | tf_op jit(solution)/shard_map/all_to_all | solution.py:21
  32.3 267.2 %all-reduce.3.cloned.1.call-start = ((), (), s32[]{:S(2)}) async-start(), calls=%async_computation.2 | async-start | bytes 8388608 | tf_op jit(solution)/shard_map/psum | solution.py:119
  160.5 3.8 copy-start.1
  161.9 4.8 collective-permute-start
  181.3 10.7 %collective-permute-start.2 = (bf16[256,512]{0,1:T(8,128)(2,1)S(1)}, bf16[256,512]{0,1:T(8,128)(2,1)S(1)}, u32[]{:S(2)}, u32[]{:S(2)}) collective-permute-start(bf16[256,512]{0,1:T(8,128)(2,1)S(1)} %slice.454), channel_id=1, source_target_pairs={{0,4},{4,0},{8,12},{12,8},{16,20},{20,16},{24,28},{28,24},{32,36},... | collective-permute-start | bytes 786440 | tf_op jit(solution)/shard_map/ppermute | solution.py:17
  188.5 3.4 collective-permute-start.1
  192.1 0.9 copy-start.2
  196.0 1.1 copy-start.3
  199.3 100.2 %all-to-all-start.1 = ((bf16[128,2,1024]{2,1,0:T(2,128)(2,1)}), bf16[128,2,1024]{2,1,0:T(2,128)(2,1)S(1)}, u32[]{:S(2)}, u32[]{:S(2)}) async-start(bf16[128,2,1024]{2,1,0:T(2,128)(2,1)} %reshape.123), calls=%async_computation.1 | async-start | bytes 1048576 | tf_op jit(solution)/shard_map/all_to_all | solution.py:21
  211.0 451.9 %all-reduce.5.cloned.1.call-start = ((), (), s32[]{:S(2)}) async-start(), calls=%async_computation.3 | async-start | bytes 8388608 | tf_op jit(solution)/shard_map/psum | solution.py:118
Sparse Core Ops, SparseCore 0:
  11.1 146.5 all-gather.3
  196.2 103.2 all-reduce.2
  303.3 359.5 all-reduce.4
